TPU v7x, 32 devices: a whole 2x2x4 slice. The times are simulated.
32 devices in a mesh: rows: 4 (over y, core), dp: 8 (over z, x).
Axes of the slice: x: 2, y: 2, z: 4, core: 2. Of those that a mesh axis runs over, the one named last changes fastest.
Arguments:
- emb_weight: float32 [8, 6144, 128], P('dp', 'rows'), may hold values from -160 to 160
- emb_grad: bfloat16 [8, 6144, 128], P('dp', 'rows'), may hold values from -6 to 6
- emb_moment: float32 [8, 6144, 128], P('dp', 'rows'), may hold values from -160 to 160
- emb_second: float32 [8, 6144, 128], P('dp', 'rows'), may hold values from 0.1 to 4
- hot_rows: int32 [8, 4, 256], P('dp', 'rows'), may hold values from 0 to 1535
- block_counts: int32 [8, 4], P('dp', 'rows'), may hold values from 1 to 2, as said below
- dense_weight: float32 [512, 256], replicated, may hold values from -8 to 8
- dense_grad: float32 [32, 512, 256], P(('rows', 'dp')), may hold values from -6 to 6
- dense_moment: float32 [512, 256], replicated, may hold values from -900 to 900
- dense_second: float32 [512, 256], replicated, may hold values from 3.2 to 128
Outputs:
- new_weight: float32 [8, 6144, 128], P('dp', 'rows')
- new_moment: float32 [8, 6144, 128], P('dp', 'rows')
- new_second: float32 [8, 6144, 128], P('dp', 'rows')
- hot_cache: bfloat16 [8, 4, 256, 128], P(None, 'rows')
- fresh_dense: float32 [512, 256], replicated
- fresh_moment: float32 [512, 256], replicated
- fresh_second: float32 [512, 256], replicated
Inputs may be any that keep to these rules, and one draw needn't show every extreme that they name: `block_counts`: some table shard has 2 live blocks in every draw. `hot_rows`: entries in dead blocks are ignored.
All inputs are finite; a program needn't handle non-finite values.
Results may differ from a plain program's by a relative error of at most 0.001.
Values may be sent and summed in bfloat16 or wider, within the bound.
A program may use at most 64 MiB of HBM per device.

v0:
```python
import jax
import jax.numpy as jnp
from jax import lax
from jax.sharding import PartitionSpec as P

BLOCK = 128
beta_one = 0.9
beta_two = 0.999
first_fix = 1.0 / (1.0 - 0.9**10)
second_fix = 1.0 / (1.0 - 0.999**10)
epsilon = 1e-06
norm_floor = 1e-06
decay_rate = 0.1
learn_rate = 0.05


def moments(gradient, moment, second):
    new_moment = beta_one * moment + (1.0 - beta_one) * gradient
    new_second = beta_two * second + (1.0 - beta_two) * gradient * gradient
    direction = first_fix * new_moment / (jnp.sqrt(second_fix * new_second) + epsilon)
    return (new_moment, new_second, direction)


def trust_step(weight_sq, update_sq):
    return learn_rate * jnp.sqrt(weight_sq + norm_floor) / jnp.sqrt(update_sq + norm_floor)


def pick_rows(source, row_ids, live_mask):
    picked = jnp.take_along_axis(source, row_ids[:, :, None], axis=1)
    return jnp.where(live_mask, picked, jnp.zeros_like(picked))


def shards(
    emb_weight,
    emb_grad,
    emb_moment,
    emb_second,
    hot_rows,
    block_counts,
    dense_weight,
    dense_grad,
    dense_moment,
    dense_second,
):
    new_moment, new_second, direction = moments(
        emb_grad.astype(jnp.float32), emb_moment, emb_second
    )
    update = direction + decay_rate * emb_weight
    weight_sq = jnp.sum(emb_weight * emb_weight, axis=(1, 2))
    update_sq = jnp.sum(update * update, axis=(1, 2))
    row_ids = hot_rows[:, 0, :]
    live_mask = (
        jnp.arange(row_ids.shape[1], dtype=jnp.int32)[None, :] < BLOCK * block_counts[:, 0][:, None]
    )[:, :, None]
    weight_sq, update_sq = lax.psum((weight_sq, update_sq), "rows")
    summed_grad = lax.psum(dense_grad[0], ("rows", "dp"))
    step_size = trust_step(weight_sq, update_sq)
    new_weight = emb_weight - step_size[:, None, None] * update
    fresh_rows = pick_rows(new_weight, row_ids, live_mask).astype(jnp.bfloat16)
    hot_cache = lax.all_gather(fresh_rows[:, None], "dp", axis=0, tiled=True)
    fresh_moment, fresh_second, heading = moments(summed_grad, dense_moment, dense_second)
    dense_scale = trust_step(jnp.sum(dense_weight * dense_weight), jnp.sum(heading * heading))
    fresh_dense = dense_weight - dense_scale * heading
    return (new_weight, new_moment, new_second, hot_cache, fresh_dense, fresh_moment, fresh_second)


def solution(mesh):
    in_specs = (
        P("dp", "rows", None),
        P("dp", "rows", None),
        P("dp", "rows", None),
        P("dp", "rows", None),
        P("dp", "rows", None),
        P("dp", "rows"),
        P(),
        P(("rows", "dp"), None, None),
        P(),
        P(),
    )
    out_specs = (
        P("dp", "rows", None),
        P("dp", "rows", None),
        P("dp", "rows", None),
        P(None, "rows", None, None),
        P(),
        P(),
        P(),
    )
    return jax.shard_map(shards, mesh=mesh, in_specs=in_specs, out_specs=out_specs, check_vma=False)
```

profile of v0, /device:TPU:0, one launch (start us, length us, event | category | flops | bytes accessed | tf_op | source)
XLA Modules:
  0.0 157.2 jit_solution(17195900723018866183)
XLA Ops:
  7.2 0.0 copy-start.7
  7.2 0.0 all-reduce.3.cloned.1.call-start
  7.2 0.7 all-reduce.3.cloned.1.call-update
  7.9 0.3 copy-done.7
  8.2 0.0 copy-start
  8.2 3.0 %multiply_reduce_fusion = (f32[]{:T(128)}, f32[]{:T(128)}, f32[1,1536,128]{2,1,0:T(8,128)S(1)}, f32[1,1536,128]{2,1,0:T(8,128)S(1)}) fusion(f32[1,1536,128]{2,1,0:T(8,128)} %param.10, bf16[1,1536,128]{2,1,0:T(8,128)(2,1)S(1)} %copy-done.7, f32[1,1536,128]{2,1,0:T(8,128)} %param.12, f32[1,1536,128]{2,1,0:T(8,128)} %param.13), kind=kLoop, calls=%fused_computation.7 | loop fusion | flops 3538942 | bytes 4325384 | tf_op jit(solution)/shard_map/reduce_sum | solution.py:50
  11.1 0.0 copy-start.1
  11.1 0.0 copy-start.2
  11.1 9.0 %all-reduce = (f32[1]{0:T(128)}, f32[1]{0:T(128)}) all-reduce(f32[1]{0:T(128)} %bitcast, f32[1]{0:T(128)} %bitcast.1), channel_id=1, replica_groups=mesh['rows'=4,'dp'=8] {'rows'}, use_global_device_ids=true, to_apply=%region_1.0 | all-reduce | flops 2 | bytes 16 | tf_op jit(solution)/shard_map/psum | solution.py:55
  21.5 0.0 copy-start.8
  21.5 0.6 copy-done.8
  22.8 0.0 copy-done
  22.8 0.4 multiply_subtract_fusion
  23.3 0.0 copy-done.1
  23.3 0.0 copy-done.2
  23.3 0.0 copy-start.3
  23.3 0.0 copy-start.4
  23.3 0.7 gather_fusion
  24.1 0.1 fusion.4
  24.2 32.1 %all_gather.3 = bf16[8,1,256,128]{3,2,1,0:T(8,128)(2,1)S(1)} all-gather(bf16[1,1,256,128]{3,2,1,0:T(8,128)(2,1)S(1)} %fusion.4), channel_id=1, replica_groups=mesh['rows'=4,'dp'=8] {'dp'}, dimensions={0}, use_global_device_ids=true | all-gather | bytes 589824 | tf_op jit(solution)/shard_map/all_gather | solution.py:60
  56.3 0.0 copy-done.4
  56.3 0.7 multiply_reduce_fusion.3
  57.0 0.0 copy-done.3
  57.7 87.8 %all-reduce.3.cloned.1.call-done = f32[512,256]{1,0:T(8,128)} async-done(((f32[512,256]{1,0:T(8,128)}), f32[512,256]{1,0:T(8,128)}) %all-reduce.3.cloned.1.call-update) | async-done | bytes 524304 | tf_op jit(solution)/shard_map/psum | solution.py:56
  145.5 2.3 %multiply_reduce_fusion.2 = (f32[]{:T(128)}, f32[512,256]{1,0:T(8,128)S(1)}, f32[512,256]{1,0:T(8,128)S(1)}) fusion(f32[512,256]{1,0:T(8,128)} %all-reduce.3.cloned.1.call-done, f32[512,256]{1,0:T(8,128)} %param.18, f32[512,256]{1,0:T(8,128)} %param.19), kind=kLoop, calls=%fused_computation.12 | loop fusion | flops 1703935 | bytes 2621444 | tf_op jit(solution)/shard_map/reduce_sum | solution.py:62
  147.8 0.0 copy-start.5
  147.8 0.0 copy-start.6
  148.5 1.0 multiply_subtract_fusion.1
  149.6 0.0 copy-done.5
  149.6 0.0 copy-done.6
  149.6 0.8 copy.21
  (3 shorter events, 0.0 us)
Async XLA Ops:
  7.2 1.0 copy-start.7
  7.2 138.3 %all-reduce.3.cloned.1.call-start = ((), (), s32[]{:S(2)}) async-start(), calls=%async_computation | async-start | bytes 1048576 | tf_op jit(solution)/shard_map/psum | solution.py:56
  8.2 14.7 %copy-start = (f32[1,1536,128]{2,1,0:T(8,128)S(1)}, f32[1,1536,128]{2,1,0:T(8,128)}, u32[]{:S(2)}) copy-start(f32[1,1536,128]{2,1,0:T(8,128)} %param.10) | copy-start | bytes 2359300
  11.1 12.2 %copy-start.1 = (f32[1,1536,128]{2,1,0:T(8,128)}, f32[1,1536,128]{2,1,0:T(8,128)S(1)}, u32[]{:S(2)}) copy-start(f32[1,1536,128]{2,1,0:T(8,128)S(1)} %get-tuple-element.26) | copy-start | bytes 2359300
  11.1 12.2 %copy-start.2 = (f32[1,1536,128]{2,1,0:T(8,128)}, f32[1,1536,128]{2,1,0:T(8,128)S(1)}, u32[]{:S(2)}) copy-start(f32[1,1536,128]{2,1,0:T(8,128)S(1)} %get-tuple-element.27) | copy-start | bytes 2359300
  21.5 0.7 copy-start.8
  23.3 33.7 %copy-start.3 = (f32[1,1536,128]{2,1,0:T(8,128)}, f32[1,1536,128]{2,1,0:T(8,128)S(1)}, u32[]{:S(2)}) copy-start(f32[1,1536,128]{2,1,0:T(8,128)S(1)} %multiply_subtract_fusion) | copy-start | bytes 2359300
  23.3 33.0 %copy-start.4 = (f32[512,256]{1,0:T(8,128)S(1)}, f32[512,256]{1,0:T(8,128)}, u32[]{:S(2)}) copy-start(f32[512,256]{1,0:T(8,128)} %param.16) | copy-start | bytes 1572868
  147.8 1.7 %copy-start.5 = (f32[512,256]{1,0:T(8,128)}, f32[512,256]{1,0:T(8,128)S(1)}, u32[]{:S(2)}) copy-start(f32[512,256]{1,0:T(8,128)S(1)} %get-tuple-element.30) | copy-start | bytes 1572868
  147.8 1.7 %copy-start.6 = (f32[512,256]{1,0:T(8,128)}, f32[512,256]{1,0:T(8,128)S(1)}, u32[]{:S(2)}) copy-start(f32[512,256]{1,0:T(8,128)S(1)} %get-tuple-element.31) | copy-start | bytes 1572868
Sparse Core Ops, SparseCore 0:
  13.3 132.1 all-reduce.2
where the time goes:
time: 158 us; the launch traced here: 157 us
  waiting for transfers between devices  88.4 us (56%)
  blocking collectives  41.1 us (26%)
  between operations  17.5 us (11%)
  other arithmetic  7.64 us (5%)
  local copies, waits for them, and re-layouts  2.46 us (2%)
    psum x1, waiting for transfers between devices, shards(): summed_grad = lax.psum(dense_grad[0], ('rows', 'dp'))  87.8 us
    all_gather x1, blocking collectives, shards(): hot_cache = lax.all_gather(fresh_rows[:, None], 'dp', axis=0, tiled=True)  32.1 us
    psum x1, blocking collectives, shards(): weight_sq, update_sq = lax.psum((weight_sq, update_sq), 'rows')  9.01 us
  transfers between devices with their start and end apart: 1, of which 1 were waited for; matrix products, arithmetic and copies ran while one was open for 3% of the time, Pallas kernels for 0%

commit v1 on v0

--- a/solution.py
+++ b/solution.py
@@ -53,7 +53,7 @@
         jnp.arange(row_ids.shape[1], dtype=jnp.int32)[None, :] < BLOCK * block_counts[:, 0][:, None]
     )[:, :, None]
     weight_sq, update_sq = lax.psum((weight_sq, update_sq), "rows")
-    summed_grad = lax.psum(dense_grad[0], ("rows", "dp"))
+    summed_grad = lax.psum(lax.psum(dense_grad[0], "dp"), "rows")
     step_size = trust_step(weight_sq, update_sq)
     new_weight = emb_weight - step_size[:, None, None] * update
     fresh_rows = pick_rows(new_weight, row_ids, live_mask).astype(jnp.bfloat16)

time: 158 us -> 134 us (0.85)
  waiting for transfers between devices: 88.4 us -> 65.4 us
    psum x1 -> x2, waiting for transfers between devices: 87.8 us -> 64.7 us  [shards(): summed_grad = lax.psum(lax.psum(dense_grad[0], 'dp'), 'rows')]
  transfers between devices with their start and end apart: 1 -> 2, of which waited for: 1 -> 2; matrix products, arithmetic and copies ran while one was open for 3% -> 4% of each run, Pallas kernels for 0% -> 0%
where the time goes in v1:
time: 134 us; the launch traced here: 133 us
  waiting for transfers between devices  65.4 us (49%)
  blocking collectives  40.6 us (30%)
  between operations  17.6 us (13%)
  other arithmetic  7.25 us (5%)
  local copies, waits for them, and re-layouts  2.41 us (2%)
    psum x2, waiting for transfers between devices, shards(): summed_grad = lax.psum(lax.psum(dense_grad[0], 'dp'), 'rows')  64.7 us
    all_gather x1, blocking collectives, shards(): hot_cache = lax.all_gather(fresh_rows[:, None], 'dp', axis=0, tiled=True)  31.6 us
    psum x1, blocking collectives, shards(): weight_sq, update_sq = lax.psum((weight_sq, update_sq), 'rows')  9.01 us
    reduce_sum x1, other arithmetic, shards(): update_sq = jnp.sum(update * update, axis=(1, 2))  2.88 us
  transfers between devices with their start and end apart: 2, of which 2 were waited for; matrix products, arithmetic and copies ran while one was open for 4% of the time, Pallas kernels for 0%

profile of v1, /device:TPU:0, one launch (start us, length us, event | category | flops | bytes accessed | tf_op | source)
XLA Modules:
  0.0 133.3 jit_solution(7645916884338954462)
XLA Ops:
  7.2 0.0 copy-start.9
  7.2 0.0 all-reduce.4.cloned.1.call-start
  7.2 0.7 all-reduce.4.cloned.1.call-update
  7.9 0.0 copy-start
  7.9 0.0 all-reduce.6.cloned.1.call-start
  8.0 0.2 copy-done.9
  8.2 2.9 %multiply_reduce_fusion = (f32[]{:T(128)}, f32[]{:T(128)}, f32[1,1536,128]{2,1,0:T(8,128)S(1)}, f32[1,1536,128]{2,1,0:T(8,128)S(1)}) fusion(f32[1,1536,128]{2,1,0:T(8,128)} %param.10, bf16[1,1536,128]{2,1,0:T(8,128)(2,1)S(1)} %copy-done.9, f32[1,1536,128]{2,1,0:T(8,128)} %param.12, f32[1,1536,128]{2,1,0:T(8,128)} %param.13), kind=kLoop, calls=%fused_computation.7 | loop fusion | flops 3538942 | bytes 4325384 | tf_op jit(solution)/shard_map/reduce_sum | solution.py:50
  11.0 0.0 copy-start.1
  11.1 0.0 copy-start.2
  11.1 9.0 %all-reduce = (f32[1]{0:T(128)}, f32[1]{0:T(128)}) all-reduce(f32[1]{0:T(128)} %bitcast, f32[1]{0:T(128)} %bitcast.1), channel_id=1, replica_groups=mesh['rows'=4,'dp'=8] {'rows'}, use_global_device_ids=true, to_apply=%region_1.0 | all-reduce | flops 2 | bytes 16 | tf_op jit(solution)/shard_map/psum | solution.py:55
  21.4 0.0 copy-start.10
  21.5 0.6 copy-done.10
  22.8 0.0 copy-done
  22.8 0.4 multiply_subtract_fusion
  23.2 0.0 copy-done.1
  23.2 0.0 copy-done.2
  23.2 0.0 copy-start.3
  23.2 0.7 gather_fusion
  24.0 0.1 fusion.4
  24.1 62.8 %all-reduce.4.cloned.1.call-done = f32[512,256]{1,0:T(8,128)} async-done(((f32[512,256]{1,0:T(8,128)}), f32[512,256]{1,0:T(8,128)}) %all-reduce.4.cloned.1.call-update) | async-done | bytes 524304 | tf_op jit(solution)/shard_map/psum | solution.py:56
  86.9 0.0 copy-start.4
  86.9 0.0 all-reduce.6.cloned.1.call-update
  87.0 0.0 copy-start.7
  87.0 0.0 copy-start.8
  87.0 31.6 %all_gather.3 = bf16[8,1,256,128]{3,2,1,0:T(8,128)(2,1)S(1)} all-gather(bf16[1,1,256,128]{3,2,1,0:T(8,128)(2,1)S(1)} %fusion.4), channel_id=1, replica_groups=mesh['rows'=4,'dp'=8] {'dp'}, dimensions={0}, use_global_device_ids=true | all-gather | bytes 589824 | tf_op jit(solution)/shard_map/all_gather | solution.py:60
  118.6 0.0 copy-done.3
  118.6 0.0 copy-done.4
  118.6 0.7 multiply_reduce_fusion.3
  120.0 1.9 %all-reduce.6.cloned.1.call-done = f32[512,256]{1,0:T(8,128)} async-done(((f32[512,256]{1,0:T(8,128)}), f32[512,256]{1,0:T(8,128)}) %all-reduce.6.cloned.1.call-update) | async-done | bytes 524304 | tf_op jit(solution)/shard_map/psum | solution.py:56
  121.9 0.0 copy-done.7
  121.9 0.0 copy-done.8
  121.9 2.0 %multiply_reduce_fusion.2 = (f32[]{:T(128)}, f32[512,256]{1,0:T(8,128)S(1)}, f32[512,256]{1,0:T(8,128)S(1)}) fusion(f32[512,256]{1,0:T(8,128)} %all-reduce.6.cloned.1.call-done, f32[512,256]{1,0:T(8,128)S(1)} %copy-done.7, f32[512,256]{1,0:T(8,128)S(1)} %copy-done.8), kind=kLoop, calls=%fused_computation.12 | loop fusion | flops 1703935 | bytes 2621444 | tf_op jit(solution)/shard_map/reduce_sum | solution.py:62
  123.9 0.0 copy-start.5
  123.9 0.0 copy-start.6
  124.6 1.0 multiply_subtract_fusion.1
  125.7 0.0 copy-done.5
  125.7 0.0 copy-done.6
  125.7 0.8 copy.22
  (3 shorter events, 0.0 us)
Async XLA Ops:
  7.2 1.0 copy-start.9
  7.2 79.8 %all-reduce.4.cloned.1.call-start = ((), (), s32[]{:S(2)}) async-start(), calls=%async_computation | async-start | bytes 1048576 | tf_op jit(solution)/shard_map/psum | solution.py:56
  7.9 14.8 %copy-start = (f32[1,1536,128]{2,1,0:T(8,128)S(1)}, f32[1,1536,128]{2,1,0:T(8,128)}, u32[]{:S(2)}) copy-start(f32[1,1536,128]{2,1,0:T(8,128)} %param.10) | copy-start | bytes 2359300
  7.9 114.0 %all-reduce.6.cloned.1.call-start = ((), (), s32[]{:S(2)}) async-start(), calls=%async_computation.1 | async-start | bytes 1048576 | tf_op jit(solution)/shard_map/psum | solution.py:56
  11.0 12.1 %copy-start.1 = (f32[1,1536,128]{2,1,0:T(8,128)}, f32[1,1536,128]{2,1,0:T(8,128)S(1)}, u32[]{:S(2)}) copy-start(f32[1,1536,128]{2,1,0:T(8,128)S(1)} %get-tuple-element.26) | copy-start | bytes 2359300
  11.1 12.1 %copy-start.2 = (f32[1,1536,128]{2,1,0:T(8,128)}, f32[1,1536,128]{2,1,0:T(8,128)S(1)}, u32[]{:S(2)}) copy-start(f32[1,1536,128]{2,1,0:T(8,128)S(1)} %get-tuple-element.27) | copy-start | bytes 2359300
  21.4 0.7 copy-start.10
  23.2 95.4 %copy-start.3 = (f32[1,1536,128]{2,1,0:T(8,128)}, f32[1,1536,128]{2,1,0:T(8,128)S(1)}, u32[]{:S(2)}) copy-start(f32[1,1536,128]{2,1,0:T(8,128)S(1)} %multiply_subtract_fusion) | copy-start | bytes 2359300
  86.9 31.6 %copy-start.4 = (f32[512,256]{1,0:T(8,128)S(1)}, f32[512,256]{1,0:T(8,128)}, u32[]{:S(2)}) copy-start(f32[512,256]{1,0:T(8,128)} %param.16) | copy-start | bytes 1572868
  87.0 34.9 %copy-start.7 = (f32[512,256]{1,0:T(8,128)S(1)}, f32[512,256]{1,0:T(8,128)}, u32[]{:S(2)}) copy-start(f32[512,256]{1,0:T(8,128)} %param.18) | copy-start | bytes 1572868
  87.0 34.9 %copy-start.8 = (f32[512,256]{1,0:T(8,128)S(1)}, f32[512,256]{1,0:T(8,128)}, u32[]{:S(2)}) copy-start(f32[512,256]{1,0:T(8,128)} %param.19) | copy-start | bytes 1572868
  123.9 1.7 %copy-start.5 = (f32[512,256]{1,0:T(8,128)}, f32[512,256]{1,0:T(8,128)S(1)}, u32[]{:S(2)}) copy-start(f32[512,256]{1,0:T(8,128)S(1)} %get-tuple-element.30) | copy-start | bytes 1572868
  123.9 1.7 %copy-start.6 = (f32[512,256]{1,0:T(8,128)}, f32[512,256]{1,0:T(8,128)S(1)}, u32[]{:S(2)}) copy-start(f32[512,256]{1,0:T(8,128)S(1)} %get-tuple-element.31) | copy-start | bytes 1572868
Sparse Core Ops, SparseCore 0:
  11.4 75.4 all-reduce.3
  89.3 32.5 all-reduce.5
